TPU v7x, 256 devices: a whole 4x4x8 slice. The times are simulated.
256 devices in a mesh: branch: 64 (over z, y, x_lo), rows: 4 (over x_hi, core).
Axes of the slice: x: 4 (x_hi: 2, x_lo: 2; x = x_hi * 2 + x_lo), y: 4, z: 8, core: 2. Of those that a mesh axis runs over, the one named last changes fastest.
Arguments:
- points: float32 [3, 524288], P(None, ('branch', 'rows')), may hold values from 0 to 1, as said below
- noise: float32 [524288], P(('branch', 'rows')), may hold values from 0.2 to 2
- landmarks: float32 [7, 3, 256], replicated, may hold values from 0 to 1, as said below
- mixing: float32 [7, 256, 256], replicated, may hold values from -6 to 6
Outputs:
- bases: float32 [3, 524288, 256], P(None, ('branch', 'rows'))
- factors: float32 [64, 3, 256, 256], P('branch')
Inputs may be any that keep to these rules, and one draw needn't show every extreme that they name: `points`: coordinates lie in the unit cube. `landmarks`: coordinates lie in the unit cube.
All inputs are finite; a program needn't handle non-finite values.
Results may differ from a plain program's by a relative error of at most 0.00025.
Values sent between devices are 32-bit elements; how exact they have to be, the bound alone decides.
A program may use at most 128 MiB of HBM per device.

v0:
```python
import jax
import jax.numpy as jnp
from jax import lax
from jax.sharding import PartitionSpec as P

highest = lax.Precision.HIGHEST


def partner(value, axis, bit):
    return lax.ppermute(value, axis, [(i, i ^ 1 << bit) for i in range(lax.axis_size(axis))])


def kernel_block(positions, landmark_set, length_scale):
    spread = jnp.zeros((positions.shape[1], landmark_set.shape[1]), jnp.float32)
    for component in range(3):
        offset = positions[component][:, None] - landmark_set[component][None, :]
        spread = spread + offset * offset
    return jnp.exp(-spread / (2.0 * length_scale * length_scale))


def project(left, right):
    return jnp.einsum(
        "nr,ns->rs", left, right, precision=highest, preferred_element_type=jnp.float32
    )


def solve_with(factor, right_side):
    return jax.scipy.linalg.cho_solve((factor, True), right_side)


def group_total(partial_value, width_bits):
    summed = lax.psum(partial_value, "rows")
    for bit_index in range(width_bits):
        summed = summed + partner(summed, "branch", bit_index)
    return summed


def on_device(points, noise, landmarks, mixing):
    width_rank = mixing.shape[1]
    local_rows = points.shape[1]
    branch_bits = lax.axis_size("branch").bit_length() - 1
    row_devices = lax.axis_size("rows")
    length_scale = 0.6 * width_rank ** (-1.0 / 3.0)
    position = lax.axis_index("branch")
    identity = jnp.eye(width_rank, dtype=jnp.float32)
    unit_list = []
    node_bits = []
    node_rows = []
    for level_index in range(3):
        width_bits = branch_bits - 2 + level_index
        node_id = 2 ** (2 - level_index) - 1 + position // 2**width_bits
        landmark_set = lax.dynamic_index_in_dim(landmarks, node_id, 0, keepdims=False)
        mixing_now = lax.dynamic_index_in_dim(mixing, node_id, 0, keepdims=False)
        kernel = kernel_block(points, landmark_set, length_scale)
        unit_list.append(
            jnp.dot(kernel, mixing_now, precision=highest, preferred_element_type=jnp.float32)
        )
        node_bits.append(width_bits)
        node_rows.append(float(2**width_bits * row_devices * local_rows))
    bases = []
    factor_list = []
    coefficients = {}
    for level_index in range(3):
        for prior_index in range(level_index):
            cross = group_total(
                project(bases[prior_index], unit_list[level_index]), node_bits[prior_index]
            )
            coefficients[prior_index, level_index] = (
                solve_with(factor_list[prior_index], cross) / node_rows[prior_index]
            )
        current = unit_list[level_index] / noise[:, None]
        for prior_index in range(level_index):
            current = current - jnp.dot(
                bases[prior_index],
                coefficients[prior_index, level_index],
                precision=highest,
                preferred_element_type=jnp.float32,
            )
        bases.append(current)
        gram_matrix = group_total(project(current, unit_list[level_index]), node_bits[level_index])
        factor = jnp.linalg.cholesky(identity + gram_matrix / node_rows[level_index])
        factor_list.append(factor)
    return (jnp.stack(bases, axis=0), jnp.stack(factor_list, axis=0)[None])


def solution(mesh):
    in_specs = (P(None, ("branch", "rows")), P(("branch", "rows")), P(), P())
    out_specs = (P(None, ("branch", "rows"), None), P("branch", None, None, None))
    return jax.shard_map(
        on_device, mesh=mesh, in_specs=in_specs, out_specs=out_specs, check_vma=False
    )
```

profile of v0, /device:TPU:8, one launch (start us, length us, event | category | flops | bytes accessed | tf_op | source)
XLA Modules:
  0.0 528.9 jit_solution(15413675945931273060)
XLA Ops:
  25.2 50.5 %all-reduce.11.cloned.1.call-done = (f32[256,256]{0,1:T(8,128)}, f32[256,256]{1,0:T(8,128)}) async-done(((f32[256,256]{0,1:T(8,128)}, f32[256,256]{1,0:T(8,128)}), (f32[256,256]{0,1:T(8,128)}, f32[256,256]{1,0:T(8,128)})) %all-reduce.11.cloned.1.call-update) | async-done | bytes 524304 | tf_op jit(solution)/shard_map/psum | solution.py:32
  77.7 7.4 %collective-permute-done = f32[256,256]{0,1:T(8,128)S(1)} collective-permute-done((f32[256,256]{0,1:T(8,128)}, f32[256,256]{0,1:T(8,128)S(1)}, u32[]{:S(2)}, u32[]{:S(2)}) %collective-permute-start) | collective-permute-done | bytes 262176 | tf_op jit(solution)/shard_map/ppermute | solution.py:10
  114.2 11.7 %cholesky.172 = f32[128,128]{1,0:T(8,128)S(1)} custom-call(f32[128,128]{1,0:T(8,128)S(1)} %cholesky.270), custom_call_target="Cholesky" | custom-call | tf_op jit(solution)/shard_map/jit(cholesky)/cholesky | solution.py:81
  126.0 9.8 %custom-call.17 = f32[1,128,128]{1,2,0:T(8,128)S(1)} custom-call(f32[1,128,128]{2,1,0:T(8,128)S(1)} %get-tuple-element.67), custom_call_target="InvertDiagBlocksLowerTriangular" | custom-call | tf_op jit(solution)/shard_map/jit(cholesky)/cholesky | solution.py:81
  136.3 11.7 %cholesky.189 = f32[128,128]{1,0:T(8,128)S(1)} custom-call(f32[128,128]{1,0:T(8,128)S(1)} %convolution_subtract_fusion.8), custom_call_target="Cholesky" | custom-call | tf_op jit(solution)/shard_map/jit(cholesky)/cholesky | solution.py:81
  154.2 19.9 %custom-call.18 = f32[2,128,128]{1,2,0:T(8,128)S(1)} custom-call(f32[2,128,128]{2,1,0:T(8,128)S(1)} %get-tuple-element.24), custom_call_target="InvertDiagBlocksLowerTriangular" | custom-call | tf_op jit(solution)/shard_map/jit(_cho_solve)/triangular_solve | solution.py:28
  189.1 47.9 %all-reduce.9.cloned.1.call-done = (f32[256,256]{1,0:T(8,128)}, f32[256,256]{1,0:T(8,128)}, f32[256,256]{0,1:T(8,128)}) async-done(((f32[256,256]{1,0:T(8,128)}, f32[256,256]{1,0:T(8,128)}, f32[256,256]{0,1:T(8,128)}), (f32[256,256]{1,0:T(8,128)}, f32[256,256]{1,0:T(8,128)}, f32[256,256]{0,1:T(8,128)})) %all-reduce.9.cloned.1.call-update) | async-done | bytes 786448 | tf_op jit(solution)/shard_map/psum | solution.py:32
  239.7 6.8 %collective-permute-done.12 = f32[256,256]{0,1:T(8,128)S(1)} collective-permute-done((f32[256,256]{0,1:T(8,128)}, f32[256,256]{0,1:T(8,128)S(1)}, u32[]{:S(2)}, u32[]{:S(2)}) %collective-permute-start.12) | collective-permute-done | bytes 262176 | tf_op jit(solution)/shard_map/ppermute | solution.py:10
  290.8 6.4 %collective-permute-done.20 = f32[256,256]{1,0:T(8,128)S(1)} collective-permute-done((f32[256,256]{1,0:T(8,128)S(1)}, f32[256,256]{1,0:T(8,128)S(1)}, u32[]{:S(2)}, u32[]{:S(2)}) %collective-permute-start.20) | collective-permute-done | bytes 262176 | tf_op jit(solution)/shard_map/ppermute | solution.py:10
  298.4 5.5 %convolution_subtract_fusion.1 = f32[2048,256]{1,0:T(8,128)} fusion(f32[2048,256]{1,0:T(8,128)} %copy-done.5, f32[2048]{0:T(1024)S(1)} %copy-done.13, f32[128,256]{0,1:T(8,128)} %copy.9, f32[128,256]{0,1:T(8,128)S(1)} %fusion.103, f32[2048,256]{1,0:T(8,128)} %copy-done.8), kind=kOutput, calls=%fused_computation.6 | convolution fusion | flops 1612316672 | bytes 6561792 | tf_op jit(solution)/shard_map/dot_general | solution.py:73
  305.1 11.7 %cholesky.206 = f32[128,128]{1,0:T(8,128)S(1)} custom-call(f32[128,128]{1,0:T(8,128)S(1)} %cholesky.273), custom_call_target="Cholesky" | custom-call | tf_op jit(solution)/shard_map/jit(cholesky)/cholesky | solution.py:81
  316.8 9.8 %custom-call.20 = f32[1,128,128]{1,2,0:T(8,128)S(1)} custom-call(f32[1,128,128]{2,1,0:T(8,128)S(1)} %get-tuple-element.63), custom_call_target="InvertDiagBlocksLowerTriangular" | custom-call | tf_op jit(solution)/shard_map/jit(cholesky)/cholesky | solution.py:81
  327.1 12.1 %cholesky.223 = f32[128,128]{1,0:T(8,128)S(1)} custom-call(f32[128,128]{1,0:T(8,128)S(1)} %convolution_subtract_fusion.7), custom_call_target="Cholesky" | custom-call | tf_op jit(solution)/shard_map/jit(cholesky)/cholesky | solution.py:81
  346.0 19.7 %custom-call.21 = f32[2,128,128]{1,2,0:T(8,128)S(1)} custom-call(f32[2,128,128]{2,1,0:T(8,128)S(1)} %get-tuple-element.26), custom_call_target="InvertDiagBlocksLowerTriangular" | custom-call | tf_op jit(solution)/shard_map/jit(_cho_solve)/triangular_solve | solution.py:28
  377.8 45.7 %all-reduce.7.cloned.1.call-done = f32[256,256]{0,1:T(8,128)} async-done(((f32[256,256]{0,1:T(8,128)}), f32[256,256]{0,1:T(8,128)}) %all-reduce.7.cloned.1.call-update) | async-done | bytes 262160 | tf_op jit(solution)/shard_map/psum | solution.py:32
  424.1 8.2 %collective-permute-done.22 = f32[256,256]{0,1:T(8,128)S(1)} collective-permute-done((f32[256,256]{0,1:T(8,128)}, f32[256,256]{0,1:T(8,128)S(1)}, u32[]{:S(2)}, u32[]{:S(2)}) %collective-permute-start.22) | collective-permute-done | bytes 262176 | tf_op jit(solution)/shard_map/ppermute | solution.py:10
  433.9 7.2 %collective-permute-done.23 = f32[256,256]{0,1:T(8,128)S(1)} collective-permute-done((f32[256,256]{0,1:T(8,128)S(1)}, f32[256,256]{0,1:T(8,128)S(1)}, u32[]{:S(2)}, u32[]{:S(2)}) %collective-permute-start.23) | collective-permute-done | bytes 262176 | tf_op jit(solution)/shard_map/ppermute | solution.py:10
  443.4 6.3 %collective-permute-done.24 = f32[256,256]{0,1:T(8,128)S(1)} collective-permute-done((f32[256,256]{0,1:T(8,128)S(1)}, f32[256,256]{0,1:T(8,128)S(1)}, u32[]{:S(2)}, u32[]{:S(2)}) %collective-permute-start.24) | collective-permute-done | bytes 262176 | tf_op jit(solution)/shard_map/ppermute | solution.py:10
  459.9 8.0 %collective-permute-done.26 = f32[256,256]{0,1:T(8,128)S(1)} collective-permute-done((f32[256,256]{0,1:T(8,128)S(1)}, f32[256,256]{0,1:T(8,128)S(1)}, u32[]{:S(2)}, u32[]{:S(2)}) %collective-permute-start.26) | collective-permute-done | bytes 262176 | tf_op jit(solution)/shard_map/ppermute | solution.py:10
  467.9 5.8 %collective-permute-start.27 = (f32[256,256]{0,1:T(8,128)S(1)}, f32[256,256]{0,1:T(8,128)S(1)}, u32[]{:S(2)}, u32[]{:S(2)}) collective-permute-start(f32[256,256]{0,1:T(8,128)S(1)} %add.201), channel_id=1, source_target_pairs={{0,128},{4,132},{8,136},{12,140},{16,144},{20,148},{24,152},{28,15... | collective-permute-start | bytes 786440 | tf_op jit(solution)/shard_map/ppermute | solution.py:10
  476.8 7.7 %collective-permute-done.27 = f32[256,256]{0,1:T(8,128)S(1)} collective-permute-done((f32[256,256]{0,1:T(8,128)S(1)}, f32[256,256]{0,1:T(8,128)S(1)}, u32[]{:S(2)}, u32[]{:S(2)}) %collective-permute-start.27) | collective-permute-done | bytes 262176 | tf_op jit(solution)/shard_map/ppermute | solution.py:10
  484.7 11.7 %cholesky.240 = f32[128,128]{1,0:T(8,128)S(1)} custom-call(f32[128,128]{1,0:T(8,128)S(1)} %cholesky.276), custom_call_target="Cholesky" | custom-call | tf_op jit(solution)/shard_map/jit(cholesky)/cholesky | solution.py:81
  496.5 9.8 %custom-call.22 = f32[1,128,128]{1,2,0:T(8,128)S(1)} custom-call(f32[1,128,128]{2,1,0:T(8,128)S(1)} %get-tuple-element.59), custom_call_target="InvertDiagBlocksLowerTriangular" | custom-call | tf_op jit(solution)/shard_map/jit(cholesky)/cholesky | solution.py:81
  506.8 11.7 %cholesky.257 = f32[128,128]{1,0:T(8,128)S(1)} custom-call(f32[128,128]{1,0:T(8,128)S(1)} %convolution_subtract_fusion.6), custom_call_target="Cholesky" | custom-call | tf_op jit(solution)/shard_map/jit(cholesky)/cholesky | solution.py:81
  (196 shorter events, 165.4 us)
Async XLA Ops:
  7.2 68.5 %all-reduce.11.cloned.1.call-start = ((), (), s32[]{:S(2)}) async-start(), calls=%async_computation.2 | async-start | bytes 1048576 | tf_op jit(solution)/shard_map/psum | solution.py:32
  25.2 211.9 %all-reduce.9.cloned.1.call-start = ((), (), s32[]{:S(2)}) async-start(), calls=%async_computation.1 | async-start | bytes 1572864 | tf_op jit(solution)/shard_map/psum | solution.py:32
  75.7 9.4 %collective-permute-start = (f32[256,256]{0,1:T(8,128)}, f32[256,256]{0,1:T(8,128)S(1)}, u32[]{:S(2)}, u32[]{:S(2)}) collective-permute-start(f32[256,256]{0,1:T(8,128)} %get-tuple-element.46), channel_id=1, source_target_pairs={{0,4},{4,0},{8,12},{12,8},{16,20},{20,16},{24,28},{28,24},{32,36},... | collective-permute-start | bytes 786440 | tf_op jit(solution)/shard_map/ppermute | solution.py:10
  76.3 13.9 %collective-permute-start.4 = (f32[256,256]{1,0:T(8,128)}, f32[256,256]{1,0:T(8,128)S(1)}, u32[]{:S(2)}, u32[]{:S(2)}) collective-permute-start(f32[256,256]{1,0:T(8,128)} %get-tuple-element.47), channel_id=1, source_target_pairs={{0,4},{4,0},{8,12},{12,8},{16,20},{20,16},{24,28},{28,24},{32,36},... | collective-permute-start | bytes 786440 | tf_op jit(solution)/shard_map/ppermute | solution.py:10
  91.1 9.3 %collective-permute-start.5 = (f32[256,256]{1,0:T(8,128)S(1)}, f32[256,256]{1,0:T(8,128)S(1)}, u32[]{:S(2)}, u32[]{:S(2)}) collective-permute-start(f32[256,256]{1,0:T(8,128)S(1)} %add.175), channel_id=1, source_target_pairs={{0,8},{4,12},{8,0},{12,4},{16,24},{20,28},{24,16},{28,20},{32,40},... | collective-permute-start | bytes 786440 | tf_op jit(solution)/shard_map/ppermute | solution.py:10
  93.3 13.6 %collective-permute-start.2 = (f32[256,256]{0,1:T(8,128)S(1)}, f32[256,256]{0,1:T(8,128)S(1)}, u32[]{:S(2)}, u32[]{:S(2)}) collective-permute-start(f32[256,256]{0,1:T(8,128)S(1)} %add.171), channel_id=1, source_target_pairs={{0,16},{4,20},{8,24},{12,28},{16,0},{20,4},{24,8},{28,12},{32,48},... | collective-permute-start | bytes 786440 | tf_op jit(solution)/shard_map/ppermute | solution.py:10
  100.4 12.8 %collective-permute-start.6 = (f32[256,256]{1,0:T(8,128)S(1)}, f32[256,256]{1,0:T(8,128)S(1)}, u32[]{:S(2)}, u32[]{:S(2)}) collective-permute-start(f32[256,256]{1,0:T(8,128)S(1)} %add.176), channel_id=1, source_target_pairs={{0,16},{4,20},{8,24},{12,28},{16,0},{20,4},{24,8},{28,12},{32,48},... | collective-permute-start | bytes 786440 | tf_op jit(solution)/shard_map/ppermute | solution.py:10
  113.3 60.8 %collective-permute-start.7 = (f32[256,256]{1,0:T(8,128)S(1)}, f32[256,256]{1,0:T(8,128)S(1)}, u32[]{:S(2)}, u32[]{:S(2)}) collective-permute-start(f32[256,256]{1,0:T(8,128)S(1)} %add.177), channel_id=1, source_target_pairs={{0,32},{4,36},{8,40},{12,44},{16,48},{20,52},{24,56},{28,60},{32,0... | collective-permute-start | bytes 786440 | tf_op jit(solution)/shard_map/ppermute | solution.py:10
  189.1 234.4 %all-reduce.7.cloned.1.call-start = ((), (), s32[]{:S(2)}) async-start(), calls=%async_computation | async-start | bytes 524288 | tf_op jit(solution)/shard_map/psum | solution.py:32
  237.1 9.4 %collective-permute-start.12 = (f32[256,256]{0,1:T(8,128)}, f32[256,256]{0,1:T(8,128)S(1)}, u32[]{:S(2)}, u32[]{:S(2)}) collective-permute-start(f32[256,256]{0,1:T(8,128)} %get-tuple-element.45), channel_id=1, source_target_pairs={{0,4},{4,0},{8,12},{12,8},{16,20},{20,16},{24,28},{28,24},{32,36},... | collective-permute-start | bytes 786440 | tf_op jit(solution)/shard_map/ppermute | solution.py:10
  237.7 14.4 %collective-permute-start.8 = (f32[256,256]{1,0:T(8,128)}, f32[256,256]{1,0:T(8,128)S(1)}, u32[]{:S(2)}, u32[]{:S(2)}) collective-permute-start(f32[256,256]{1,0:T(8,128)} %get-tuple-element.43), channel_id=1, source_target_pairs={{0,4},{4,0},{8,12},{12,8},{16,20},{20,16},{24,28},{28,24},{32,36},... | collective-permute-start | bytes 786440 | tf_op jit(solution)/shard_map/ppermute | solution.py:10
  239.1 18.0 %collective-permute-start.17 = (f32[256,256]{1,0:T(8,128)}, f32[256,256]{1,0:T(8,128)S(1)}, u32[]{:S(2)}, u32[]{:S(2)}) collective-permute-start(f32[256,256]{1,0:T(8,128)} %get-tuple-element.44), channel_id=1, source_target_pairs={{0,4},{4,0},{8,12},{12,8},{16,20},{20,16},{24,28},{28,24},{32,36},... | collective-permute-start | bytes 786440 | tf_op jit(solution)/shard_map/ppermute | solution.py:10
  247.5 11.3 %collective-permute-start.13 = (f32[256,256]{0,1:T(8,128)S(1)}, f32[256,256]{0,1:T(8,128)S(1)}, u32[]{:S(2)}, u32[]{:S(2)}) collective-permute-start(f32[256,256]{0,1:T(8,128)S(1)} %add.186), channel_id=1, source_target_pairs={{0,8},{4,12},{8,0},{12,4},{16,24},{20,28},{24,16},{28,20},{32,40},... | collective-permute-start | bytes 786440 | tf_op jit(solution)/shard_map/ppermute | solution.py:10
  258.1 9.3 %collective-permute-start.18 = (f32[256,256]{1,0:T(8,128)S(1)}, f32[256,256]{1,0:T(8,128)S(1)}, u32[]{:S(2)}, u32[]{:S(2)}) collective-permute-start(f32[256,256]{1,0:T(8,128)S(1)} %add.192), channel_id=1, source_target_pairs={{0,8},{4,12},{8,0},{12,4},{16,24},{20,28},{24,16},{28,20},{32,40},... | collective-permute-start | bytes 786440 | tf_op jit(solution)/shard_map/ppermute | solution.py:10
  258.8 15.1 %collective-permute-start.14 = (f32[256,256]{0,1:T(8,128)S(1)}, f32[256,256]{0,1:T(8,128)S(1)}, u32[]{:S(2)}, u32[]{:S(2)}) collective-permute-start(f32[256,256]{0,1:T(8,128)S(1)} %add.187), channel_id=1, source_target_pairs={{0,16},{4,20},{8,24},{12,28},{16,0},{20,4},{24,8},{28,12},{32,48},... | collective-permute-start | bytes 786440 | tf_op jit(solution)/shard_map/ppermute | solution.py:10
  261.3 18.2 %collective-permute-start.10 = (f32[256,256]{1,0:T(8,128)S(1)}, f32[256,256]{1,0:T(8,128)S(1)}, u32[]{:S(2)}, u32[]{:S(2)}) collective-permute-start(f32[256,256]{1,0:T(8,128)S(1)} %add.183), channel_id=1, source_target_pairs={{0,16},{4,20},{8,24},{12,28},{16,0},{20,4},{24,8},{28,12},{32,48},... | collective-permute-start | bytes 786440 | tf_op jit(solution)/shard_map/ppermute | solution.py:10
  267.4 16.7 %collective-permute-start.19 = (f32[256,256]{1,0:T(8,128)S(1)}, f32[256,256]{1,0:T(8,128)S(1)}, u32[]{:S(2)}, u32[]{:S(2)}) collective-permute-start(f32[256,256]{1,0:T(8,128)S(1)} %add.193), channel_id=1, source_target_pairs={{0,16},{4,20},{8,24},{12,28},{16,0},{20,4},{24,8},{28,12},{32,48},... | collective-permute-start | bytes 786440 | tf_op jit(solution)/shard_map/ppermute | solution.py:10
  274.0 11.8 %collective-permute-start.15 = (f32[256,256]{0,1:T(8,128)S(1)}, f32[256,256]{0,1:T(8,128)S(1)}, u32[]{:S(2)}, u32[]{:S(2)}) collective-permute-start(f32[256,256]{0,1:T(8,128)S(1)} %add.188), channel_id=1, source_target_pairs={{0,32},{4,36},{8,40},{12,44},{16,48},{20,52},{24,56},{28,60},{32,0... | collective-permute-start | bytes 786440 | tf_op jit(solution)/shard_map/ppermute | solution.py:10
  279.6 8.9 %collective-permute-start.11 = (f32[256,256]{1,0:T(8,128)S(1)}, f32[256,256]{1,0:T(8,128)S(1)}, u32[]{:S(2)}, u32[]{:S(2)}) collective-permute-start(f32[256,256]{1,0:T(8,128)S(1)} %add.184), channel_id=1, source_target_pairs={{0,32},{4,36},{8,40},{12,44},{16,48},{20,52},{24,56},{28,60},{32,0... | collective-permute-start | bytes 786440 | tf_op jit(solution)/shard_map/ppermute | solution.py:10
  284.1 13.0 %collective-permute-start.20 = (f32[256,256]{1,0:T(8,128)S(1)}, f32[256,256]{1,0:T(8,128)S(1)}, u32[]{:S(2)}, u32[]{:S(2)}) collective-permute-start(f32[256,256]{1,0:T(8,128)S(1)} %add.194), channel_id=1, source_target_pairs={{0,32},{4,36},{8,40},{12,44},{16,48},{20,52},{24,56},{28,60},{32,0... | collective-permute-start | bytes 786440 | tf_op jit(solution)/shard_map/ppermute | solution.py:10
  285.8 18.0 %collective-permute-start.16 = (f32[256,256]{0,1:T(8,128)S(1)}, f32[256,256]{0,1:T(8,128)}, u32[]{:S(2)}, u32[]{:S(2)}) collective-permute-start(f32[256,256]{0,1:T(8,128)S(1)} %add.189), channel_id=1, source_target_pairs={{0,64},{4,68},{8,72},{12,76},{16,80},{20,84},{24,88},{28,92},{32,9... | collective-permute-start | bytes 786440 | tf_op jit(solution)/shard_map/ppermute | solution.py:10
  297.2 68.5 %collective-permute-start.21 = (f32[256,256]{1,0:T(8,128)S(1)}, f32[256,256]{1,0:T(8,128)S(1)}, u32[]{:S(2)}, u32[]{:S(2)}) collective-permute-start(f32[256,256]{1,0:T(8,128)S(1)} %add.195), channel_id=1, source_target_pairs={{0,64},{4,68},{8,72},{12,76},{16,80},{20,84},{24,88},{28,92},{32,9... | collective-permute-start | bytes 786440 | tf_op jit(solution)/shard_map/ppermute | solution.py:10
  456.2 11.7 %collective-permute-start.26 = (f32[256,256]{0,1:T(8,128)S(1)}, f32[256,256]{0,1:T(8,128)S(1)}, u32[]{:S(2)}, u32[]{:S(2)}) collective-permute-start(f32[256,256]{0,1:T(8,128)S(1)} %add.200), channel_id=1, source_target_pairs={{0,64},{4,68},{8,72},{12,76},{16,80},{20,84},{24,88},{28,92},{32,9... | collective-permute-start | bytes 786440 | tf_op jit(solution)/shard_map/ppermute | solution.py:10
  467.9 16.6 %collective-permute-start.27 = (f32[256,256]{0,1:T(8,128)S(1)}, f32[256,256]{0,1:T(8,128)S(1)}, u32[]{:S(2)}, u32[]{:S(2)}) collective-permute-start(f32[256,256]{0,1:T(8,128)S(1)} %add.201), channel_id=1, source_target_pairs={{0,128},{4,132},{8,136},{12,140},{16,144},{20,148},{24,152},{28,15... | collective-permute-start | bytes 786440 | tf_op jit(solution)/shard_map/ppermute | solution.py:10
  (21 other events, 181.7 us)
Sparse Core Ops, SparseCore 0:
  25.3 50.3 all-reduce.10
  189.2 47.8 all-reduce.8
  378.0 45.4 all-reduce.6
where the time goes:
time: 538 us; the launch traced here: 529 us
  waiting for transfers between devices  241 us (45%)
  other arithmetic  155 us (29%)
  matrix products  55.8 us (10%)
  starting transfers between devices  44.3 us (8%)
  between operations  18.6 us (3%)
  local copies, waits for them, and re-layouts  14 us (3%)
    psum x3, waiting for transfers between devices, group_total(): summed = lax.psum(partial_value, 'rows')  144 us
    another operation x20, other arithmetic, on_device(): jnp.linalg.cholesky(identity + gram_matrix / node_rows[level_index])  104 us
    ppermute x28, waiting for transfers between devices, partner(): lax.ppermute(value, axis, [(i, i ^ 1 << bit) for i in range(lax.axis_size...  96.5 us
    ppermute x28, starting transfers between devices, partner(): lax.ppermute(value, axis, [(i, i ^ 1 << bit) for i in range(lax.axis_size...  44.2 us
    another operation x3, other arithmetic, solve_with(): return jax.scipy.linalg.cho_solve((factor, True), right_side)  39.6 us
    dot_general x6, matrix products, project(): jnp.einsum('nr,ns->rs', left, right, precision=highest, preferred_element...  27.2 us
    dot_general x3, matrix products, on_device(): jnp.dot(bases[prior_index], coefficients[prior_index, level_index], preci...  14.2 us
  transfers between devices with their start and end apart: 31, of which 22 were waited for; matrix products, arithmetic and copies ran while one was open for 27% of the time, Pallas kernels for 0%

commit v1 on v0

--- a/solution.py
+++ b/solution.py
@@ -2,6 +2,7 @@
 import jax.numpy as jnp
 from jax import lax
 from jax.sharding import PartitionSpec as P
+from jax.lax import all_gather
 
 highest = lax.Precision.HIGHEST
 
@@ -29,7 +30,8 @@
 
 
 def group_total(partial_value, width_bits):
-    summed = lax.psum(partial_value, "rows")
+    replace_terms = lambda vec: jnp.sum(all_gather(vec, "rows"), axis=0)
+    summed = replace_terms(partial_value)
     for bit_index in range(width_bits):
         summed = summed + partner(summed, "branch", bit_index)
     return summed

time: 538 us -> 483 us (0.90)
  waiting for transfers between devices: 241 us -> 187 us
    psum x3 -> x0, waiting for transfers between devices: 144 us -> none  [group_total(): summed = lax.psum(partial_value, 'rows')]
    all_gather x0 -> x6, waiting for transfers between devices: none -> 70.4 us  [group_total(): replace_terms = lambda vec: jnp.sum(all_gather(vec, 'rows'), axis=0)]
    ppermute x28, waiting for transfers between devices: 96.5 us -> 116 us  [partner(): lax.ppermute(value, axis, [(i, i ^ 1 << bit) for i in range(lax.axis_size...]
    reduce_sum x0 -> x6, other arithmetic: none -> 7.94 us  [group_total(): replace_terms = lambda vec: jnp.sum(all_gather(vec, 'rows'), axis=0)]
  transfers between devices with their start and end apart: 31 -> 34, of which waited for: 22 -> 23; matrix products, arithmetic and copies ran while one was open for 27% -> 35% of each run, Pallas kernels for 0% -> 0%
where the time goes in v1:
time: 483 us; the launch traced here: 478 us
  waiting for transfers between devices  187 us (39%)
  other arithmetic  158 us (33%)
  matrix products  57.3 us (12%)
  starting transfers between devices  40.4 us (8%)
  between operations  19 us (4%)
  local copies, waits for them, and re-layouts  16.2 us (3%)
    ppermute x28, waiting for transfers between devices, partner(): lax.ppermute(value, axis, [(i, i ^ 1 << bit) for i in range(lax.axis_size...  116 us
    another operation x20, other arithmetic, on_device(): jnp.linalg.cholesky(identity + gram_matrix / node_rows[level_index])  103 us
    all_gather x6, waiting for transfers between devices, group_total(): replace_terms = lambda vec: jnp.sum(all_gather(vec, 'rows'), axis=0)  70.4 us
    ppermute x28, starting transfers between devices, partner(): lax.ppermute(value, axis, [(i, i ^ 1 << bit) for i in range(lax.axis_size...  39.7 us
    another operation x3, other arithmetic, solve_with(): return jax.scipy.linalg.cho_solve((factor, True), right_side)  39.4 us
    dot_general x6, matrix products, project(): jnp.einsum('nr,ns->rs', left, right, precision=highest, preferred_element...  28.8 us
    dot_general x3, matrix products, on_device(): jnp.dot(bases[prior_index], coefficients[prior_index, level_index], preci...  14.1 us
  transfers between devices with their start and end apart: 34, of which 23 were waited for; matrix products, arithmetic and copies ran while one was open for 35% of the time, Pallas kernels for 0%

profile of v1, /device:TPU:8, one launch (start us, length us, event | category | flops | bytes accessed | tf_op | source)
XLA Modules:
  0.0 477.8 jit_solution(7492827573289778706)
XLA Ops:
  26.3 17.6 %all-gather.13.cloned.1.call-done = f32[1024,256]{1,0:T(8,128)} async-done(((f32[256,256]{1,0:T(8,128)}), f32[1024,256]{1,0:T(8,128)}) %all-gather.13.cloned.1.call-update) | async-done | bytes 1048592 | tf_op jit(solution)/shard_map/all_gather | solution.py:33
  46.0 23.1 %all-gather.15.cloned.1.call-done = f32[1024,256]{1,0:T(8,128)} async-done(((f32[256,256]{1,0:T(8,128)}), f32[1024,256]{1,0:T(8,128)}) %all-gather.15.cloned.1.call-update) | async-done | bytes 1048592 | tf_op jit(solution)/shard_map/all_gather | solution.py:33
  71.7 7.2 %collective-permute-done.4 = f32[256,256]{1,0:T(8,128)S(1)} collective-permute-done((f32[256,256]{1,0:T(8,128)S(1)}, f32[256,256]{1,0:T(8,128)S(1)}, u32[]{:S(2)}, u32[]{:S(2)}) %collective-permute-start.4) | collective-permute-done | bytes 262176 | tf_op jit(solution)/shard_map/ppermute | solution.py:11
  102.4 11.7 %cholesky.172 = f32[128,128]{1,0:T(8,128)S(1)} custom-call(f32[128,128]{1,0:T(8,128)S(1)} %cholesky.270), custom_call_target="Cholesky" | custom-call | tf_op jit(solution)/shard_map/jit(cholesky)/cholesky | solution.py:83
  114.2 9.8 %custom-call.17 = f32[1,128,128]{1,2,0:T(8,128)S(1)} custom-call(f32[1,128,128]{2,1,0:T(8,128)S(1)} %get-tuple-element.62), custom_call_target="InvertDiagBlocksLowerTriangular" | custom-call | tf_op jit(solution)/shard_map/jit(cholesky)/cholesky | solution.py:83
  124.5 11.7 %cholesky.189 = f32[128,128]{1,0:T(8,128)S(1)} custom-call(f32[128,128]{1,0:T(8,128)S(1)} %convolution_subtract_fusion.8), custom_call_target="Cholesky" | custom-call | tf_op jit(solution)/shard_map/jit(cholesky)/cholesky | solution.py:83
  142.5 19.7 %custom-call.18 = f32[2,128,128]{1,2,0:T(8,128)S(1)} custom-call(f32[2,128,128]{2,1,0:T(8,128)S(1)} %get-tuple-element.24), custom_call_target="InvertDiagBlocksLowerTriangular" | custom-call | tf_op jit(solution)/shard_map/jit(_cho_solve)/triangular_solve | solution.py:29
  182.9 8.0 %collective-permute-done.8 = f32[256,256]{1,0:T(8,128)S(1)} collective-permute-done((f32[256,256]{1,0:T(8,128)S(1)}, f32[256,256]{1,0:T(8,128)S(1)}, u32[]{:S(2)}, u32[]{:S(2)}) %collective-permute-start.8) | collective-permute-done | bytes 262176 | tf_op jit(solution)/shard_map/ppermute | solution.py:11
  199.9 7.9 %collective-permute-done.10 = f32[256,256]{1,0:T(8,128)S(1)} collective-permute-done((f32[256,256]{1,0:T(8,128)S(1)}, f32[256,256]{1,0:T(8,128)S(1)}, u32[]{:S(2)}, u32[]{:S(2)}) %collective-permute-start.10) | collective-permute-done | bytes 262176 | tf_op jit(solution)/shard_map/ppermute | solution.py:11
  215.3 8.2 %all-gather.21.cloned.1.call-done = f32[1024,256]{1,0:T(8,128)} async-done(((f32[256,256]{1,0:T(8,128)}), f32[1024,256]{1,0:T(8,128)}) %all-gather.21.cloned.1.call-update) | async-done | bytes 1048592 | tf_op jit(solution)/shard_map/all_gather | solution.py:33
  235.4 7.3 %collective-permute-done.18 = f32[256,256]{1,0:T(8,128)S(1)} collective-permute-done((f32[256,256]{1,0:T(8,128)S(1)}, f32[256,256]{1,0:T(8,128)S(1)}, u32[]{:S(2)}, u32[]{:S(2)}) %collective-permute-start.18) | collective-permute-done | bytes 262176 | tf_op jit(solution)/shard_map/ppermute | solution.py:11
  268.5 9.8 %collective-permute-done.16 = f32[256,256]{0,1:T(8,128)S(1)} collective-permute-done((f32[256,256]{0,1:T(8,128)S(1)}, f32[256,256]{0,1:T(8,128)S(1)}, u32[]{:S(2)}, u32[]{:S(2)}) %collective-permute-start.16) | collective-permute-done | bytes 262176 | tf_op jit(solution)/shard_map/ppermute | solution.py:11
  278.5 11.7 %cholesky.206 = f32[128,128]{1,0:T(8,128)S(1)} custom-call(f32[128,128]{1,0:T(8,128)S(1)} %cholesky.273), custom_call_target="Cholesky" | custom-call | tf_op jit(solution)/shard_map/jit(cholesky)/cholesky | solution.py:83
  290.3 9.8 %custom-call.20 = f32[1,128,128]{1,2,0:T(8,128)S(1)} custom-call(f32[1,128,128]{2,1,0:T(8,128)S(1)} %get-tuple-element.58), custom_call_target="InvertDiagBlocksLowerTriangular" | custom-call | tf_op jit(solution)/shard_map/jit(cholesky)/cholesky | solution.py:83
  300.6 11.7 %cholesky.223 = f32[128,128]{1,0:T(8,128)S(1)} custom-call(f32[128,128]{1,0:T(8,128)S(1)} %convolution_subtract_fusion.7), custom_call_target="Cholesky" | custom-call | tf_op jit(solution)/shard_map/jit(cholesky)/cholesky | solution.py:83
  319.1 19.7 %custom-call.21 = f32[2,128,128]{1,2,0:T(8,128)S(1)} custom-call(f32[2,128,128]{2,1,0:T(8,128)S(1)} %get-tuple-element.26), custom_call_target="InvertDiagBlocksLowerTriangular" | custom-call | tf_op jit(solution)/shard_map/jit(_cho_solve)/triangular_solve | solution.py:29
  350.9 21.6 %all-gather.23.cloned.1.call-done = f32[1024,256]{1,0:T(8,128)} async-done(((f32[256,256]{1,0:T(8,128)}), f32[1024,256]{1,0:T(8,128)}) %all-gather.23.cloned.1.call-update) | async-done | bytes 1048592 | tf_op jit(solution)/shard_map/all_gather | solution.py:33
  374.6 7.9 %collective-permute-done.22 = f32[256,256]{0,1:T(8,128)S(1)} collective-permute-done((f32[256,256]{0,1:T(8,128)S(1)}, f32[256,256]{0,1:T(8,128)S(1)}, u32[]{:S(2)}, u32[]{:S(2)}) %collective-permute-start.22) | collective-permute-done | bytes 262176 | tf_op jit(solution)/shard_map/ppermute | solution.py:11
  383.2 7.0 %collective-permute-done.23 = f32[256,256]{0,1:T(8,128)S(1)} collective-permute-done((f32[256,256]{0,1:T(8,128)S(1)}, f32[256,256]{0,1:T(8,128)S(1)}, u32[]{:S(2)}, u32[]{:S(2)}) %collective-permute-start.23) | collective-permute-done | bytes 262176 | tf_op jit(solution)/shard_map/ppermute | solution.py:11
  408.9 7.7 %collective-permute-done.26 = f32[256,256]{0,1:T(8,128)S(1)} collective-permute-done((f32[256,256]{0,1:T(8,128)S(1)}, f32[256,256]{0,1:T(8,128)S(1)}, u32[]{:S(2)}, u32[]{:S(2)}) %collective-permute-start.26) | collective-permute-done | bytes 262176 | tf_op jit(solution)/shard_map/ppermute | solution.py:11
  425.6 7.5 %collective-permute-done.27 = f32[256,256]{0,1:T(8,128)S(1)} collective-permute-done((f32[256,256]{0,1:T(8,128)S(1)}, f32[256,256]{0,1:T(8,128)S(1)}, u32[]{:S(2)}, u32[]{:S(2)}) %collective-permute-start.27) | collective-permute-done | bytes 262176 | tf_op jit(solution)/shard_map/ppermute | solution.py:11
  433.4 11.7 %cholesky.240 = f32[128,128]{1,0:T(8,128)S(1)} custom-call(f32[128,128]{1,0:T(8,128)S(1)} %cholesky.276), custom_call_target="Cholesky" | custom-call | tf_op jit(solution)/shard_map/jit(cholesky)/cholesky | solution.py:83
  445.2 9.8 %custom-call.22 = f32[1,128,128]{1,2,0:T(8,128)S(1)} custom-call(f32[1,128,128]{2,1,0:T(8,128)S(1)} %get-tuple-element.54), custom_call_target="InvertDiagBlocksLowerTriangular" | custom-call | tf_op jit(solution)/shard_map/jit(cholesky)/cholesky | solution.py:83
  455.5 11.7 %cholesky.257 = f32[128,128]{1,0:T(8,128)S(1)} custom-call(f32[128,128]{1,0:T(8,128)S(1)} %convolution_subtract_fusion.6), custom_call_target="Cholesky" | custom-call | tf_op jit(solution)/shard_map/jit(cholesky)/cholesky | solution.py:83
  (214 shorter events, 186.9 us)
Async XLA Ops:
  7.2 36.7 %all-gather.13.cloned.1.call-start = ((), (), s32[]{:S(2)}) async-start(), calls=%async_computation | async-start | bytes 1310720 | tf_op jit(solution)/shard_map/all_gather | solution.py:33
  17.6 51.5 %all-gather.15.cloned.1.call-start = ((), (), s32[]{:S(2)}) async-start(), calls=%async_computation.1 | async-start | bytes 1310720 | tf_op jit(solution)/shard_map/all_gather | solution.py:33
  26.3 154.7 %all-gather.17.cloned.1.call-start = ((), (), s32[]{:S(2)}) async-start(), calls=%async_computation.2 | async-start | bytes 1310720 | tf_op jit(solution)/shard_map/all_gather | solution.py:33
  45.4 25.7 %collective-permute-start = (f32[256,256]{0,1:T(8,128)S(1)}, f32[256,256]{0,1:T(8,128)S(1)}, u32[]{:S(2)}, u32[]{:S(2)}) collective-permute-start(f32[256,256]{0,1:T(8,128)S(1)} %copy.13), channel_id=1, source_target_pairs={{0,4},{4,0},{8,12},{12,8},{16,20},{20,16},{24,28},{28,24},{32,36},... | collective-permute-start | bytes 786440 | tf_op jit(solution)/shard_map/ppermute | solution.py:11
  79.0 9.3 %collective-permute-start.5 = (f32[256,256]{1,0:T(8,128)S(1)}, f32[256,256]{1,0:T(8,128)S(1)}, u32[]{:S(2)}, u32[]{:S(2)}) collective-permute-start(f32[256,256]{1,0:T(8,128)S(1)} %add.163), channel_id=1, source_target_pairs={{0,8},{4,12},{8,0},{12,4},{16,24},{20,28},{24,16},{28,20},{32,40},... | collective-permute-start | bytes 786440 | tf_op jit(solution)/shard_map/ppermute | solution.py:11
  79.6 15.1 %collective-permute-start.2 = (f32[256,256]{0,1:T(8,128)S(1)}, f32[256,256]{0,1:T(8,128)S(1)}, u32[]{:S(2)}, u32[]{:S(2)}) collective-permute-start(f32[256,256]{0,1:T(8,128)S(1)} %add.159), channel_id=1, source_target_pairs={{0,16},{4,20},{8,24},{12,28},{16,0},{20,4},{24,8},{28,12},{32,48},... | collective-permute-start | bytes 786440 | tf_op jit(solution)/shard_map/ppermute | solution.py:11
  88.3 12.9 %collective-permute-start.6 = (f32[256,256]{1,0:T(8,128)S(1)}, f32[256,256]{1,0:T(8,128)S(1)}, u32[]{:S(2)}, u32[]{:S(2)}) collective-permute-start(f32[256,256]{1,0:T(8,128)S(1)} %add.164), channel_id=1, source_target_pairs={{0,16},{4,20},{8,24},{12,28},{16,0},{20,4},{24,8},{28,12},{32,48},... | collective-permute-start | bytes 786440 | tf_op jit(solution)/shard_map/ppermute | solution.py:11
  101.1 108.4 %all-gather.19.cloned.1.call-start = ((), (), s32[]{:S(2)}) async-start(), calls=%async_computation.3 | async-start | bytes 1310720 | tf_op jit(solution)/shard_map/all_gather | solution.py:33
  101.2 61.0 %collective-permute-start.7 = (f32[256,256]{1,0:T(8,128)S(1)}, f32[256,256]{1,0:T(8,128)S(1)}, u32[]{:S(2)}, u32[]{:S(2)}) collective-permute-start(f32[256,256]{1,0:T(8,128)S(1)} %add.165), channel_id=1, source_target_pairs={{0,32},{4,36},{8,40},{12,44},{16,48},{20,52},{24,56},{28,60},{32,0... | collective-permute-start | bytes 786440 | tf_op jit(solution)/shard_map/ppermute | solution.py:11
  174.2 49.3 %all-gather.21.cloned.1.call-start = ((), (), s32[]{:S(2)}) async-start(), calls=%async_computation.4 | async-start | bytes 1310720 | tf_op jit(solution)/shard_map/all_gather | solution.py:33
  180.9 191.6 %all-gather.23.cloned.1.call-start = ((), (), s32[]{:S(2)}) async-start(), calls=%async_computation.5 | async-start | bytes 1310720 | tf_op jit(solution)/shard_map/all_gather | solution.py:33
  182.3 8.7 %collective-permute-start.8 = (f32[256,256]{1,0:T(8,128)S(1)}, f32[256,256]{1,0:T(8,128)S(1)}, u32[]{:S(2)}, u32[]{:S(2)}) collective-permute-start(f32[256,256]{1,0:T(8,128)S(1)} %reduce_sum.56), channel_id=1, source_target_pairs={{0,4},{4,0},{8,12},{12,8},{16,20},{20,16},{24,28},{28,24},{32,36},... | collective-permute-start | bytes 786440 | tf_op jit(solution)/shard_map/ppermute | solution.py:11
  191.0 8.7 %collective-permute-start.9 = (f32[256,256]{1,0:T(8,128)S(1)}, f32[256,256]{1,0:T(8,128)S(1)}, u32[]{:S(2)}, u32[]{:S(2)}) collective-permute-start(f32[256,256]{1,0:T(8,128)S(1)} %add.170), channel_id=1, source_target_pairs={{0,8},{4,12},{8,0},{12,4},{16,24},{20,28},{24,16},{28,20},{32,40},... | collective-permute-start | bytes 786440 | tf_op jit(solution)/shard_map/ppermute | solution.py:11
  210.9 14.2 %collective-permute-start.12 = (f32[256,256]{0,1:T(8,128)S(1)}, f32[256,256]{0,1:T(8,128)S(1)}, u32[]{:S(2)}, u32[]{:S(2)}) collective-permute-start(f32[256,256]{0,1:T(8,128)S(1)} %copy.18), channel_id=1, source_target_pairs={{0,4},{4,0},{8,12},{12,8},{16,20},{20,16},{24,28},{28,24},{32,36},... | collective-permute-start | bytes 786440 | tf_op jit(solution)/shard_map/ppermute | solution.py:11
  225.2 8.6 %collective-permute-start.13 = (f32[256,256]{0,1:T(8,128)S(1)}, f32[256,256]{0,1:T(8,128)S(1)}, u32[]{:S(2)}, u32[]{:S(2)}) collective-permute-start(f32[256,256]{0,1:T(8,128)S(1)} %add.174), channel_id=1, source_target_pairs={{0,8},{4,12},{8,0},{12,4},{16,24},{20,28},{24,16},{28,20},{32,40},... | collective-permute-start | bytes 786440 | tf_op jit(solution)/shard_map/ppermute | solution.py:11
  233.4 9.3 %collective-permute-start.18 = (f32[256,256]{1,0:T(8,128)S(1)}, f32[256,256]{1,0:T(8,128)S(1)}, u32[]{:S(2)}, u32[]{:S(2)}) collective-permute-start(f32[256,256]{1,0:T(8,128)S(1)} %add.180), channel_id=1, source_target_pairs={{0,8},{4,12},{8,0},{12,4},{16,24},{20,28},{24,16},{28,20},{32,40},... | collective-permute-start | bytes 786440 | tf_op jit(solution)/shard_map/ppermute | solution.py:11
  233.9 13.5 %collective-permute-start.14 = (f32[256,256]{0,1:T(8,128)S(1)}, f32[256,256]{0,1:T(8,128)S(1)}, u32[]{:S(2)}, u32[]{:S(2)}) collective-permute-start(f32[256,256]{0,1:T(8,128)S(1)} %add.175), channel_id=1, source_target_pairs={{0,16},{4,20},{8,24},{12,28},{16,0},{20,4},{24,8},{28,12},{32,48},... | collective-permute-start | bytes 786440 | tf_op jit(solution)/shard_map/ppermute | solution.py:11
  242.7 8.7 %collective-permute-start.19 = (f32[256,256]{1,0:T(8,128)S(1)}, f32[256,256]{1,0:T(8,128)S(1)}, u32[]{:S(2)}, u32[]{:S(2)}) collective-permute-start(f32[256,256]{1,0:T(8,128)S(1)} %add.181), channel_id=1, source_target_pairs={{0,16},{4,20},{8,24},{12,28},{16,0},{20,4},{24,8},{28,12},{32,48},... | collective-permute-start | bytes 786440 | tf_op jit(solution)/shard_map/ppermute | solution.py:11
  247.5 11.0 %collective-permute-start.15 = (f32[256,256]{0,1:T(8,128)S(1)}, f32[256,256]{0,1:T(8,128)}, u32[]{:S(2)}, u32[]{:S(2)}) collective-permute-start(f32[256,256]{0,1:T(8,128)S(1)} %add.176), channel_id=1, source_target_pairs={{0,32},{4,36},{8,40},{12,44},{16,48},{20,52},{24,56},{28,60},{32,0... | collective-permute-start | bytes 786440 | tf_op jit(solution)/shard_map/ppermute | solution.py:11
  251.5 13.5 %collective-permute-start.20 = (f32[256,256]{1,0:T(8,128)S(1)}, f32[256,256]{1,0:T(8,128)S(1)}, u32[]{:S(2)}, u32[]{:S(2)}) collective-permute-start(f32[256,256]{1,0:T(8,128)S(1)} %add.182), channel_id=1, source_target_pairs={{0,32},{4,36},{8,40},{12,44},{16,48},{20,52},{24,56},{28,60},{32,0... | collective-permute-start | bytes 786440 | tf_op jit(solution)/shard_map/ppermute | solution.py:11
  259.5 18.8 %collective-permute-start.16 = (f32[256,256]{0,1:T(8,128)S(1)}, f32[256,256]{0,1:T(8,128)S(1)}, u32[]{:S(2)}, u32[]{:S(2)}) collective-permute-start(f32[256,256]{0,1:T(8,128)S(1)} %add.177), channel_id=1, source_target_pairs={{0,64},{4,68},{8,72},{12,76},{16,80},{20,84},{24,88},{28,92},{32,9... | collective-permute-start | bytes 786440 | tf_op jit(solution)/shard_map/ppermute | solution.py:11
  265.0 73.8 %collective-permute-start.21 = (f32[256,256]{1,0:T(8,128)S(1)}, f32[256,256]{1,0:T(8,128)S(1)}, u32[]{:S(2)}, u32[]{:S(2)}) collective-permute-start(f32[256,256]{1,0:T(8,128)S(1)} %add.183), channel_id=1, source_target_pairs={{0,64},{4,68},{8,72},{12,76},{16,80},{20,84},{24,88},{28,92},{32,9... | collective-permute-start | bytes 786440 | tf_op jit(solution)/shard_map/ppermute | solution.py:11
  405.1 11.5 %collective-permute-start.26 = (f32[256,256]{0,1:T(8,128)S(1)}, f32[256,256]{0,1:T(8,128)S(1)}, u32[]{:S(2)}, u32[]{:S(2)}) collective-permute-start(f32[256,256]{0,1:T(8,128)S(1)} %add.188), channel_id=1, source_target_pairs={{0,64},{4,68},{8,72},{12,76},{16,80},{20,84},{24,88},{28,92},{32,9... | collective-permute-start | bytes 786440 | tf_op jit(solution)/shard_map/ppermute | solution.py:11
  416.7 16.5 %collective-permute-start.27 = (f32[256,256]{0,1:T(8,128)S(1)}, f32[256,256]{0,1:T(8,128)S(1)}, u32[]{:S(2)}, u32[]{:S(2)}) collective-permute-start(f32[256,256]{0,1:T(8,128)S(1)} %add.189), channel_id=1, source_target_pairs={{0,128},{4,132},{8,136},{12,140},{16,144},{20,148},{24,152},{28,15... | collective-permute-start | bytes 786440 | tf_op jit(solution)/shard_map/ppermute | solution.py:11
  (24 other events, 199.9 us)
Sparse Core Ops, SparseCore 0:
  17.7 26.1 all-gather.12
  46.3 22.7 all-gather.14
  101.2 20.9 all-gather.16
  174.3 22.0 all-gather.18
  198.1 25.3 all-gather.20
  351.1 21.3 all-gather.22
